TPU v7x, 512 devices: a whole 4x8x8 slice. The times are simulated.
512 devices in a mesh: req: 64 (over x, y, core), tp: 8 (over z).
Axes of the slice: x: 4, y: 8, z: 8, core: 2. Of those that a mesh axis runs over, the one named last changes fastest.
Arguments:
- queries: bfloat16 [64, 28, 4096], P('req', None, 'tp'), may hold values from -25 to 25
- tree_kv: bfloat16 [64, 28, 2048], P('req', None, 'tp'), may hold values from -4 to 4
- tree_parent: int32 [64, 28], P('req'), may hold values from -1 to 26, as said below
- accepted_path: int32 [64, 8], replicated, may hold values from -1 to 27, as said below
- cache_kv: bfloat16 [192, 256, 2048], P('req', None, 'tp'), may hold values from -6 to 6
- piece_owner: int32 [192, 2], P('req'), may hold values from -1 to 63, as said below
- cache_len: int32 [64], replicated, may hold values from 1 to 1016, as said below
- out_weight: bfloat16 [4096, 4096], P('tp', 'req'), may hold values from -0.09375 to 0.09375
Outputs:
- mixed: bfloat16 [64, 28, 4096], P('tp', None, 'req')
- cache_out: bfloat16 [192, 256, 2048], P('req', None, 'tp')
Inputs may be any that keep to these rules, and one draw needn't show every extreme that they name: tree_parent[r, 0] = -1 and 0 <= tree_parent[r, i] < i for i >= 1; tokens 1 to 7 have parent i - 1. accepted_path[r] lists, root first, the tokens on the path from token 0 to some token of request r's tree, then -1 entries; it holds 1 to 8 tokens, and 8 for some request. piece_owner[s] = (r, p) means slot s holds cache rows p * 256 to p * 256 + 255 of request r; (-1, -1) marks an unused slot. For each request r the pieces 0 to (cache_len[r] + 7) // 256 stand in exactly one slot each, and no other pieces do. cache_len[r] + 8 <= 1024.
All inputs are finite; a program needn't handle non-finite values.
Results may differ from a plain program's by a relative error of at most 0.02.
Values may be sent and summed in bfloat16 or wider, within the bound.
No kernel may reach another device: no remote copies, remote signals or barrier semaphores. Data moves between devices by JAX's collectives and lax.ppermute only.
A program may use at most 64 MiB of HBM per device.

v0:
```python
import math
import jax
import jax.numpy as jnp
from jax import lax
from jax.sharding import PartitionSpec as P

HD = 128
NEG = -1e30


def ancestors(parent):
    tree_size = parent.shape[-1]
    node_ids = lax.broadcasted_iota(jnp.int32, (tree_size, tree_size), 1)
    parent_hot = (parent[..., :, None] == node_ids).astype(jnp.float32)
    reached = jnp.minimum(parent_hot + jnp.eye(tree_size, dtype=jnp.float32), 1.0)
    for rounds in range(max(1, (tree_size - 1).bit_length())):
        reached = jnp.minimum(
            jnp.einsum("rij,rjk->rik", reached, reached, precision=lax.Precision.HIGHEST), 1.0
        )
    return reached


def shards(
    queries, tree_kv, tree_parent, accepted_path, cache_kv, piece_owner, cache_len, out_weight
):
    kvheads_local = tree_kv.shape[-1] // (2 * HD)
    heads_local = queries.shape[-1] // HD
    group_size = heads_local // kvheads_local
    tree_size = queries.shape[1]
    slot_count = cache_kv.shape[0]
    piece_rows = cache_kv.shape[1]
    depth_most = accepted_path.shape[1]
    scaling = 1.0 / math.sqrt(HD)
    every_query = lax.all_gather(queries, "req", axis=0, tiled=True)
    req_total = every_query.shape[0]
    owner_req = piece_owner[:, 0]
    owner_piece = piece_owner[:, 1]
    safe_req = jnp.maximum(owner_req, 0)
    slot_query = every_query[safe_req].reshape(slot_count, tree_size, kvheads_local, group_size, HD)
    stored = cache_kv.reshape(slot_count, piece_rows, kvheads_local, 2, HD)
    row_pos = owner_piece[:, None] * piece_rows + lax.broadcasted_iota(
        jnp.int32, (slot_count, piece_rows), 1
    )
    visible = (owner_req >= 0)[:, None] & (row_pos < cache_len[safe_req][:, None])
    wide_mask = visible[:, None, None, None, :]
    scores = (
        jnp.einsum(
            "stkgd,spkd->stkgp", slot_query, stored[:, :, :, 0], preferred_element_type=jnp.float32
        )
        * scaling
    )
    scores = jnp.where(wide_mask, scores, NEG)
    slot_peak = jnp.max(scores, -1)
    expo = jnp.where(wide_mask, jnp.exp(scores - slot_peak[..., None]), 0.0)
    slot_den = jnp.sum(expo, -1)
    weights = expo.astype(jnp.bfloat16)
    slot_num = jnp.einsum(
        "stkgp,spkd->stkgd", weights, stored[:, :, :, 1], preferred_element_type=jnp.float32
    )
    request_ids = lax.broadcasted_iota(jnp.int32, (req_total, slot_count), 0)
    member = (owner_req[None, :] == request_ids)[:, :, None, None, None]
    req_peak = jnp.max(jnp.where(member, slot_peak[None], NEG), axis=1)
    factor = jnp.where(
        member, jnp.exp(jnp.where(member, slot_peak[None] - req_peak[:, None], 0.0)), 0.0
    )
    req_den = jnp.sum(factor * slot_den[None], axis=1)
    req_num = jnp.einsum("rstkg,stkgd->rtkgd", factor, slot_num, precision=lax.Precision.HIGHEST)
    peak_table = req_peak.reshape(req_total, tree_size, heads_local)
    den_table = req_den.reshape(req_total, tree_size, heads_local)
    num_table = req_num.reshape(req_total, tree_size, heads_local * HD)
    own_index = lax.axis_index("req")
    got_peak, got_den, got_num = (
        lax.all_to_all(
            peak_table.astype(jnp.bfloat16), "req", split_axis=0, concat_axis=0, tiled=True
        ).astype(peak_table.dtype),
        lax.all_to_all(
            den_table.astype(jnp.bfloat16), "req", split_axis=0, concat_axis=0, tiled=True
        ).astype(den_table.dtype),
        lax.all_to_all(
            num_table.astype(jnp.bfloat16), "req", split_axis=0, concat_axis=0, tiled=True
        ).astype(num_table.dtype),
    )
    cache_peak = jnp.max(got_peak, axis=0)
    source_scale = jnp.exp(got_peak - cache_peak[None])
    cache_den = jnp.sum(source_scale * got_den, axis=0)
    got_rows = got_num.reshape(got_num.shape[0], tree_size, heads_local, HD)
    cache_num = jnp.sum(source_scale[..., None] * got_rows, axis=0)
    reached = ancestors(tree_parent)[0]
    home_query = queries[0].reshape(tree_size, kvheads_local, group_size, HD)
    fresh = tree_kv[0].reshape(tree_size, kvheads_local, 2, HD)
    tree_mask = reached[:, None, None, :] > 0.5
    tree_scores = (
        jnp.einsum("ikgd,jkd->ikgj", home_query, fresh[:, :, 0], preferred_element_type=jnp.float32)
        * scaling
    )
    tree_scores = jnp.where(tree_mask, tree_scores, NEG)
    tree_peak = jnp.max(tree_scores, -1)
    tree_exp = jnp.where(tree_mask, jnp.exp(tree_scores - tree_peak[..., None]), 0.0)
    tree_den = jnp.sum(tree_exp, -1).reshape(tree_size, heads_local)
    tree_num = jnp.einsum(
        "ikgj,jkd->ikgd",
        tree_exp.astype(jnp.bfloat16),
        fresh[:, :, 1],
        preferred_element_type=jnp.float32,
    )
    tree_num = tree_num.reshape(tree_size, heads_local, HD)
    tree_peak = tree_peak.reshape(tree_size, heads_local)
    total_peak = jnp.maximum(cache_peak, tree_peak)
    cache_scale = jnp.exp(cache_peak - total_peak)
    tree_scale = jnp.exp(tree_peak - total_peak)
    denom = cache_den * cache_scale + tree_den * tree_scale
    numer = cache_num * cache_scale[..., None] + tree_num * tree_scale[..., None]
    attention = (
        (numer / denom[..., None]).reshape(1, tree_size, heads_local * HD).astype(jnp.bfloat16)
    )
    piece = lax.all_gather(attention, "req", axis=0, tiled=True)
    flat_rows = piece.reshape(piece.shape[0] * piece.shape[1], piece.shape[2])
    product = jnp.dot(flat_rows, out_weight, preferred_element_type=jnp.float32)
    terms = product.reshape(piece.shape[0], piece.shape[1], out_weight.shape[1])
    mixed = lax.psum_scatter(terms.astype(jnp.bfloat16), "tp", scatter_dimension=0, tiled=True)
    own_path = lax.dynamic_index_in_dim(accepted_path, own_index, 0, keepdims=False)
    picked = tree_kv[0][jnp.maximum(own_path, 0)]
    picked = jnp.where((own_path >= 0)[:, None], picked, jnp.zeros_like(picked))
    all_rows = lax.all_gather(picked[None], "req", axis=0, tiled=True)
    counts = jnp.sum((accepted_path >= 0).astype(jnp.int32), axis=1)
    offset = row_pos - cache_len[safe_req][:, None]
    writing = (owner_req >= 0)[:, None] & (offset >= 0) & (offset < counts[safe_req][:, None])
    slot_rows = all_rows[safe_req]
    chosen = jnp.take_along_axis(slot_rows, jnp.clip(offset, 0, depth_most - 1)[:, :, None], axis=1)
    cache_out = jnp.where(writing[:, :, None], chosen, cache_kv)
    return (mixed, cache_out)


def solution(mesh):
    return jax.shard_map(
        shards,
        mesh=mesh,
        in_specs=(
            P("req", None, "tp"),
            P("req", None, "tp"),
            P("req", None),
            P(),
            P("req", None, "tp"),
            P("req", None),
            P(),
            P("tp", "req"),
        ),
        out_specs=(P("tp", None, "req"), P("req", None, "tp")),
        check_vma=False,
    )
```

profile of v0, /device:TPU:2, one launch (start us, length us, event | category | flops | bytes accessed | tf_op | source)
XLA Modules:
  0.0 331.0 jit_solution(16705288890588195445)
XLA Ops:
  7.2 0.7 all-gather.3.cloned.1.call-update
  7.9 1.2 copy.126
  9.1 0.8 slice_bitcast_fusion.4
  9.9 0.7 convert_reduce_fusion
  10.6 0.6 gather_fusion.2
  11.2 1.3 gather_fusion
  12.6 0.7 compare_bitcast_fusion
  13.3 84.3 %all-gather.3.cloned.1.call-done = bf16[64,28,512]{2,1,0:T(8,128)(2,1)} async-done(((bf16[1,28,512]{2,1,0:T(8,128)(2,1)}), bf16[64,28,512]{2,1,0:T(8,128)(2,1)}) %all-gather.3.cloned.1.call-update) | async-done | bytes 1835024 | tf_op jit(solution)/shard_map/all_gather | solution.py:34
  97.6 2.1 gather_fusion.1
  100.9 0.8 copy.130
  101.7 8.0 %all-to-all-start = ((bf16[64,28,4]{1,2,0:T(4,128)(2,1)}), bf16[64,28,4]{1,2,0:T(4,128)(2,1)S(1)}, u32[]{:S(2)}, u32[]{:S(2)}) async-start(bf16[64,28,4]{1,2,0:T(4,128)(2,1)} %copy.130), calls=%async_computation | async-start | bytes 131072 | tf_op jit(solution)/shard_map/all_to_all | solution.py:73
  110.2 0.8 copy.151
  110.9 7.5 %all-to-all-done = bf16[64,28,4]{1,2,0:T(4,128)(2,1)S(1)} async-done(((bf16[64,28,4]{1,2,0:T(4,128)(2,1)}), bf16[64,28,4]{1,2,0:T(4,128)(2,1)S(1)}, u32[]{:S(2)}, u32[]{:S(2)}) %all-to-all-start) | async-done | bytes 14368 | tf_op jit(solution)/shard_map/all_to_all | solution.py:73
  118.5 5.5 %all-to-all-start.2 = ((bf16[64,28,4]{1,2,0:T(4,128)(2,1)}), bf16[64,28,4]{1,2,0:T(4,128)(2,1)S(1)}, u32[]{:S(2)}, u32[]{:S(2)}) async-start(bf16[64,28,4]{1,2,0:T(4,128)(2,1)} %copy.151), calls=%async_computation.2 | async-start | bytes 131072 | tf_op jit(solution)/shard_map/all_to_all | solution.py:76
  124.0 6.0 %convert_bitcast_fusion = bf16[64,28,1,4,128]{4,0,3,1,2:T(8,128)(2,1)S(1)} fusion(f32[3,28,4,128]{3,1,2,0:T(8,128)S(1)} %fusion.19, f32[64,28,4]{0,2,1:T(4,128)S(1)} %select_reduce_fusion, f32[3,28,4]{0,2,1:T(4,128)S(1)} %copy.137, pred[64,3]{0,1:T(4,128)(4,1)S(1)} %iota_compare_fusion), kind=kOutput, calls=%fused_computation.9 | convolution fusion | flops 34012160 | bytes 2037248 | tf_op jit(solution)/shard_map/rstkg,stkgd->rtkgd/dot_general | solution.py:67
  130.0 1.4 copy.161
  131.4 1.8 reshape.676
  133.3 10.7 %all-to-all-start.1 = ((bf16[64,28,512]{2,1,0:T(8,128)(2,1)}), bf16[64,28,512]{2,1,0:T(8,128)(2,1)S(1)}, u32[]{:S(2)}, u32[]{:S(2)}) async-start(bf16[64,28,512]{2,1,0:T(8,128)(2,1)} %reshape.676), calls=%async_computation.1 | async-start | bytes 4194304 | tf_op jit(solution)/shard_map/all_to_all | solution.py:79
  147.0 3.5 %mul.113 = f32[64,28,4,128]{3,2,0,1:T(4,128)} broadcast(f32[64,28,4]{2,0,1:T(8,128)S(1)} %copy.135), dimensions={0,1,2} | broadcast | bytes 3698688 | tf_op jit(solution)/shard_map/mul | solution.py:87
  150.5 5.2 %mul.114 = f32[64,28,512]{2,0,1:T(8,128)} reshape(f32[64,28,4,128]{3,2,0,1:T(4,128)} %mul.113) | data formatting | bytes 7340032 | tf_op jit(solution)/shard_map/mul | solution.py:87
  155.7 37.8 %all-to-all-done.1 = bf16[64,28,512]{2,1,0:T(8,128)(2,1)S(1)} async-done(((bf16[64,28,512]{2,1,0:T(8,128)(2,1)}), bf16[64,28,512]{2,1,0:T(8,128)(2,1)S(1)}, u32[]{:S(2)}, u32[]{:S(2)}) %all-to-all-start.1) | async-done | bytes 1835040 | tf_op jit(solution)/shard_map/all_to_all | solution.py:79
  193.5 3.6 %multiply_reduce_fusion = f32[28,512]{1,0:T(8,128)S(1)} fusion(f32[64,28,512]{2,0,1:T(8,128)} %mul.114, bf16[64,28,512]{2,1,0:T(8,128)(2,1)S(1)} %all-to-all-done.1), kind=kLoop, calls=%fused_computation.6 | loop fusion | flops 2738176 | bytes 5562368 | tf_op jit(solution)/shard_map/reduce_sum | solution.py:87
  197.5 0.6 copy.156
  199.2 37.4 %all_gather.11 = bf16[64,8,256]{2,1,0:T(8,128)(2,1)S(1)} all-gather(bf16[1,8,256]{2,1,0:T(8,128)(2,1)S(1)} %bitcast_select_fusion), channel_id=1, replica_groups=mesh['req'=64,'tp'=8] {'req'}, dimensions={0}, use_global_device_ids=true | all-gather | bytes 266240 | tf_op jit(solution)/shard_map/all_gather | solution.py:124
  237.2 41.2 %all-gather.5.cloned.1.call-done = bf16[64,28,512]{2,1,0:T(8,128)(2,1)} async-done(((bf16[1,28,512]{2,1,0:T(8,128)(2,1)}), bf16[64,28,512]{2,1,0:T(8,128)(2,1)}) %all-gather.5.cloned.1.call-update) | async-done | bytes 1835024 | tf_op jit(solution)/shard_map/all_gather | solution.py:116
  278.4 3.7 %fusion.2 = bf16[64,28,64]{2,0,1:T(8,128)(2,1)S(1)} fusion(bf16[64,28,512]{2,1,0:T(8,128)(2,1)} %all-gather.5.cloned.1.call-done, bf16[512,64]{0,1:T(8,128)(2,1)S(1)} %copy-done), kind=kOutput, calls=%fused_computation.10 | convolution fusion | flops 117555200 | bytes 2129920 | tf_op jit(solution)/shard_map/dot_general | solution.py:118
  282.4 1.1 reshape.677
  283.7 4.2 %gather_fusion.5 = bf16[768,256]{1,0:T(8,128)(2,1)S(1)} fusion(bf16[3,8,256]{2,1,0:T(8,128)(2,1)S(1)} %gather_fusion.4, s32[768]{0:T(1024)S(1)} %reshape.664), kind=kCustom, calls=%fused_computation.5 | custom fusion | bytes 792576 | tf_op jit(solution)/shard_map/jit(take_along_axis)/gather | solution.py:129
  287.9 1.0 select_select_fusion
  288.9 34.0 %reduce-scatter.4.cloned.1.call-done = bf16[8,1792]{1,0:T(8,128)(2,1)} async-done(((bf16[64,1792]{1,0:T(8,128)(2,1)}), bf16[8,1792]{1,0:T(8,128)(2,1)}) %reduce-scatter.4.cloned.1.call-update) | async-done | bytes 28688
  322.9 0.9 reshape.678
  323.8 0.6 copy.163
  (69 shorter events, 7.2 us)
Async XLA Ops:
  7.2 271.3 %copy-start = (bf16[512,64]{0,1:T(8,128)(2,1)S(1)}, bf16[512,64]{0,1:T(8,128)(2,1)}, u32[]{:S(2)}) copy-start(bf16[512,64]{0,1:T(8,128)(2,1)} %param.15) | copy-start | bytes 196612
  7.2 90.4 %all-gather.3.cloned.1.call-start = ((), (), s32[]{:S(2)}) async-start(), calls=%async_computation.4 | async-start | bytes 2129920 | tf_op jit(solution)/shard_map/all_gather | solution.py:34
  101.7 16.8 %all-to-all-start = ((bf16[64,28,4]{1,2,0:T(4,128)(2,1)}), bf16[64,28,4]{1,2,0:T(4,128)(2,1)S(1)}, u32[]{:S(2)}, u32[]{:S(2)}) async-start(bf16[64,28,4]{1,2,0:T(4,128)(2,1)} %copy.130), calls=%async_computation | async-start | bytes 131072 | tf_op jit(solution)/shard_map/all_to_all | solution.py:73
  118.5 14.8 %all-to-all-start.2 = ((bf16[64,28,4]{1,2,0:T(4,128)(2,1)}), bf16[64,28,4]{1,2,0:T(4,128)(2,1)S(1)}, u32[]{:S(2)}, u32[]{:S(2)}) async-start(bf16[64,28,4]{1,2,0:T(4,128)(2,1)} %copy.151), calls=%async_computation.2 | async-start | bytes 131072 | tf_op jit(solution)/shard_map/all_to_all | solution.py:76
  133.3 10.7 %copy-start.3 = (bf16[1,28,512]{2,1,0:T(8,128)(2,1)S(1)}, bf16[1,28,512]{2,1,0:T(8,128)(2,1)}, u32[]{:S(2)}) copy-start(bf16[1,28,512]{2,1,0:T(8,128)(2,1)} %param.8) | copy-start | bytes 86020
  133.3 10.8 %copy-start.2 = (bf16[1,28,256]{2,1,0:T(8,128)(2,1)S(1)}, bf16[1,28,256]{2,1,0:T(8,128)(2,1)}, u32[]{:S(2)}) copy-start(bf16[1,28,256]{2,1,0:T(8,128)(2,1)} %param.9) | copy-start | bytes 43012
  133.3 10.8 %copy-start.5 = (s32[1,28]{1,0:T(1,128)S(1)}, s32[1,28]{1,0:T(1,128)}, u32[]{:S(2)}) copy-start(s32[1,28]{1,0:T(1,128)} %param.10) | copy-start | bytes 340
  133.3 60.2 %all-to-all-start.1 = ((bf16[64,28,512]{2,1,0:T(8,128)(2,1)}), bf16[64,28,512]{2,1,0:T(8,128)(2,1)S(1)}, u32[]{:S(2)}, u32[]{:S(2)}) async-start(bf16[64,28,512]{2,1,0:T(8,128)(2,1)} %reshape.676), calls=%async_computation.1 | async-start | bytes 4194304 | tf_op jit(solution)/shard_map/all_to_all | solution.py:79
  143.9 134.5 %all-gather.5.cloned.1.call-start = ((), (), s32[]{:S(2)}) async-start(), calls=%async_computation.5 | async-start | bytes 2129920 | tf_op jit(solution)/shard_map/all_gather | solution.py:116
  155.7 42.5 %copy-start.4 = (s32[64,8]{0,1:T(8,128)S(1)}, s32[64,8]{0,1:T(8,128)}, u32[]{:S(2)}) copy-start(s32[64,8]{0,1:T(8,128)} %param.11) | copy-start | bytes 6148
  198.1 124.8 %reduce-scatter.4.cloned.1.call-start = ((), (), s32[]{:S(2)}) async-start(), calls=%async_computation.6 | async-start | bytes 258048
  283.6 4.3 %copy-start.1 = (bf16[3,256,256]{2,1,0:T(8,128)(2,1)S(1)}, bf16[3,256,256]{2,1,0:T(8,128)(2,1)}, u32[]{:S(2)}) copy-start(bf16[3,256,256]{2,1,0:T(8,128)(2,1)} %param.12) | copy-start | bytes 1179652
Sparse Core Ops, SparseCore 0:
  11.4 86.1 all-gather.2
  198.3 80.1 all-gather.4
  283.7 39.1 reduce-scatter.3
where the time goes:
time: 332 us; the launch traced here: 331 us
  waiting for transfers between devices  206 us (62%)
  blocking collectives  37.4 us (11%)
  local copies, waits for them, and re-layouts  29.6 us (9%)
  starting transfers between devices  24.3 us (7%)
  between operations  14.1 us (4%)
  matrix products  11.4 us (3%)
  other arithmetic  8.73 us (3%)
    all_gather x1, waiting for transfers between devices, shards(): every_query = lax.all_gather(queries, 'req', axis=0, tiled=True)  84.3 us
    all_gather x1, waiting for transfers between devices, shards(): piece = lax.all_gather(attention, 'req', axis=0, tiled=True)  41.2 us
    all_to_all x1, waiting for transfers between devices, shards(): lax.all_to_all(num_table.astype(jnp.bfloat16), 'req', split_axis=0, conca...  37.8 us
    all_gather x1, blocking collectives, shards(): all_rows = lax.all_gather(picked[None], 'req', axis=0, tiled=True)  37.4 us
    unnamed x4, waiting for transfers between devices  34.7 us
    all_to_all x1, starting transfers between devices, shards(): lax.all_to_all(num_table.astype(jnp.bfloat16), 'req', split_axis=0, conca...  10.7 us
    mul x2, local copies, waits for them, and re-layouts, shards(): cache_num = jnp.sum(source_scale[..., None] * got_rows, axis=0)  8.76 us
    all_to_all x1, starting transfers between devices, shards(): lax.all_to_all(peak_table.astype(jnp.bfloat16), 'req', split_axis=0, conc...  7.97 us
  transfers between devices with their start and end apart: 6, of which 5 were waited for; matrix products, arithmetic and copies ran while one was open for 10% of the time, Pallas kernels for 0%

commit v1 on v0

--- a/solution.py
+++ b/solution.py
@@ -6,6 +6,12 @@
 
 HD = 128
 NEG = -1e30
+
+
+def gather_from_all(x, axis, dim):
+    count = lax.axis_size(axis)
+    repeats = [count if d == dim else 1 for d in range(x.ndim)]
+    return lax.all_to_all(jnp.tile(x, repeats), axis, split_axis=dim, concat_axis=dim, tiled=True)
 
 
 def ancestors(parent):
@@ -31,7 +37,7 @@
     piece_rows = cache_kv.shape[1]
     depth_most = accepted_path.shape[1]
     scaling = 1.0 / math.sqrt(HD)
-    every_query = lax.all_gather(queries, "req", axis=0, tiled=True)
+    every_query = gather_from_all(queries, "req", 0)
     req_total = every_query.shape[0]
     owner_req = piece_owner[:, 0]
     owner_piece = piece_owner[:, 1]

time: 332 us -> 305 us (0.919)
  waiting for transfers between devices: 206 us -> 167 us
  starting transfers between devices: 24.3 us -> 34.6 us
    all_gather x1 -> x0, waiting for transfers between devices: 84.3 us -> none  [shards(): every_query = lax.all_gather(queries, 'req', axis=0, tiled=True)]
    all_to_all x0 -> x1, waiting for transfers between devices: none -> 47.2 us  [gather_from_all(): lax.all_to_all(jnp.tile(x, repeats), axis, split_axis=dim, concat_axis=di...]
    all_to_all x0 -> x1, starting transfers between devices: none -> 10.8 us  [gather_from_all(): lax.all_to_all(jnp.tile(x, repeats), axis, split_axis=dim, concat_axis=di...]
    all_to_all x1, waiting for transfers between devices: 37.8 us -> 34.4 us  [shards(): lax.all_to_all(num_table.astype(jnp.bfloat16), 'req', split_axis=0, conca...]
    unnamed x4 -> x3, waiting for transfers between devices: 34.7 us -> 34 us
  transfers between devices with their start and end apart: 6 -> 6, of which waited for: 5 -> 5; matrix products, arithmetic and copies ran while one was open for 10% -> 11% of each run, Pallas kernels for 0% -> 0%
where the time goes in v1:
time: 305 us; the launch traced here: 304 us
  waiting for transfers between devices  167 us (55%)
  blocking collectives  37.4 us (12%)
  starting transfers between devices  34.6 us (11%)
  local copies, waits for them, and re-layouts  31.4 us (10%)
  between operations  14.5 us (5%)
  matrix products  11.3 us (4%)
  other arithmetic  7.49 us (2%)
    all_to_all x1, waiting for transfers between devices, gather_from_all(): lax.all_to_all(jnp.tile(x, repeats), axis, split_axis=dim, concat_axis=di...  47.2 us
    all_gather x1, waiting for transfers between devices, shards(): piece = lax.all_gather(attention, 'req', axis=0, tiled=True)  44.1 us
    all_gather x1, blocking collectives, shards(): all_rows = lax.all_gather(picked[None], 'req', axis=0, tiled=True)  37.4 us
    all_to_all x1, waiting for transfers between devices, shards(): lax.all_to_all(num_table.astype(jnp.bfloat16), 'req', split_axis=0, conca...  34.4 us
    unnamed x3, waiting for transfers between devices  34 us
    all_to_all x1, starting transfers between devices, gather_from_all(): lax.all_to_all(jnp.tile(x, repeats), axis, split_axis=dim, concat_axis=di...  10.8 us
    all_to_all x1, starting transfers between devices, shards(): lax.all_to_all(num_table.astype(jnp.bfloat16), 'req', split_axis=0, conca...  10.5 us
    mul x2, local copies, waits for them, and re-layouts, shards(): cache_num = jnp.sum(source_scale[..., None] * got_rows, axis=0)  8.76 us
  transfers between devices with their start and end apart: 6, of which 5 were waited for; matrix products, arithmetic and copies ran while one was open for 11% of the time, Pallas kernels for 0%

profile of v1, /device:TPU:2, one launch (start us, length us, event | category | flops | bytes accessed | tf_op | source)
XLA Modules:
  0.0 304.1 jit_solution(15334267616857455319)
XLA Ops:
  7.2 2.4 tile.10
  9.6 10.8 %all-to-all-start = ((bf16[64,28,512]{2,1,0:T(8,128)(2,1)}), bf16[64,28,512]{2,1,0:T(8,128)(2,1)S(1)}, u32[]{:S(2)}, u32[]{:S(2)}) async-start(bf16[64,28,512]{2,1,0:T(8,128)(2,1)} %tile.10), calls=%async_computation | async-start | bytes 4194304 | tf_op jit(solution)/shard_map/all_to_all | solution.py:14
  21.3 0.6 gather_fusion
  22.0 0.7 fusion.50
  22.7 47.2 %all-to-all-done = bf16[64,28,512]{2,1,0:T(8,128)(2,1)S(1)} async-done(((bf16[64,28,512]{2,1,0:T(8,128)(2,1)}), bf16[64,28,512]{2,1,0:T(8,128)(2,1)S(1)}, u32[]{:S(2)}, u32[]{:S(2)}) %all-to-all-start) | async-done | bytes 1835040 | tf_op jit(solution)/shard_map/all_to_all | solution.py:14
  71.7 0.8 copy.129
  72.4 7.5 %all-to-all-start.1 = ((bf16[64,28,4]{1,2,0:T(4,128)(2,1)}), bf16[64,28,4]{1,2,0:T(4,128)(2,1)S(1)}, u32[]{:S(2)}, u32[]{:S(2)}) async-start(bf16[64,28,4]{1,2,0:T(4,128)(2,1)} %copy.129), calls=%async_computation.1 | async-start | bytes 131072 | tf_op jit(solution)/shard_map/all_to_all | solution.py:79
  80.5 0.8 copy.150
  81.2 7.5 %all-to-all-done.1 = bf16[64,28,4]{1,2,0:T(4,128)(2,1)S(1)} async-done(((bf16[64,28,4]{1,2,0:T(4,128)(2,1)}), bf16[64,28,4]{1,2,0:T(4,128)(2,1)S(1)}, u32[]{:S(2)}, u32[]{:S(2)}) %all-to-all-start.1) | async-done | bytes 14368 | tf_op jit(solution)/shard_map/all_to_all | solution.py:79
  88.8 5.5 %all-to-all-start.3 = ((bf16[64,28,4]{1,2,0:T(4,128)(2,1)}), bf16[64,28,4]{1,2,0:T(4,128)(2,1)S(1)}, u32[]{:S(2)}, u32[]{:S(2)}) async-start(bf16[64,28,4]{1,2,0:T(4,128)(2,1)} %copy.150), calls=%async_computation.3 | async-start | bytes 131072 | tf_op jit(solution)/shard_map/all_to_all | solution.py:82
  94.3 6.0 %convert_bitcast_fusion = bf16[64,28,1,4,128]{4,0,3,1,2:T(8,128)(2,1)S(1)} fusion(f32[3,28,4,128]{3,1,2,0:T(8,128)S(1)} %fusion.19, f32[64,28,4]{0,2,1:T(4,128)S(1)} %select_reduce_fusion, f32[3,28,4]{0,2,1:T(4,128)S(1)} %copy.136, pred[64,3]{0,1:T(4,128)(4,1)S(1)} %iota_compare_fusion), kind=kOutput, calls=%fused_computation.9 | convolution fusion | flops 34012160 | bytes 2037248 | tf_op jit(solution)/shard_map/rstkg,stkgd->rtkgd/dot_general | solution.py:73
  100.3 1.4 copy.160
  101.7 1.8 reshape.679
  103.6 10.5 %all-to-all-start.2 = ((bf16[64,28,512]{2,1,0:T(8,128)(2,1)}), bf16[64,28,512]{2,1,0:T(8,128)(2,1)S(1)}, u32[]{:S(2)}, u32[]{:S(2)}) async-start(bf16[64,28,512]{2,1,0:T(8,128)(2,1)} %reshape.679), calls=%async_computation.2 | async-start | bytes 4194304 | tf_op jit(solution)/shard_map/all_to_all | solution.py:85
  116.3 0.7 subtract_exponential_fusion
  117.2 0.7 copy.154
  117.9 0.7 copy.148
  118.6 0.7 copy.144
  119.2 1.2 copy.134
  120.4 3.5 %mul.113 = f32[64,28,4,128]{3,2,0,1:T(4,128)} broadcast(f32[64,28,4]{2,0,1:T(8,128)S(1)} %copy.134), dimensions={0,1,2} | broadcast | bytes 3698688 | tf_op jit(solution)/shard_map/mul | solution.py:93
  124.0 5.2 %mul.114 = f32[64,28,512]{2,0,1:T(8,128)} reshape(f32[64,28,4,128]{3,2,0,1:T(4,128)} %mul.113) | data formatting | bytes 7340032 | tf_op jit(solution)/shard_map/mul | solution.py:93
  129.2 34.4 %all-to-all-done.2 = bf16[64,28,512]{2,1,0:T(8,128)(2,1)S(1)} async-done(((bf16[64,28,512]{2,1,0:T(8,128)(2,1)}), bf16[64,28,512]{2,1,0:T(8,128)(2,1)S(1)}, u32[]{:S(2)}, u32[]{:S(2)}) %all-to-all-start.2) | async-done | bytes 1835040 | tf_op jit(solution)/shard_map/all_to_all | solution.py:85
  163.6 3.3 %multiply_reduce_fusion = f32[28,512]{1,0:T(8,128)S(1)} fusion(f32[64,28,512]{2,0,1:T(8,128)} %mul.114, bf16[64,28,512]{2,1,0:T(8,128)(2,1)S(1)} %all-to-all-done.2), kind=kLoop, calls=%fused_computation.6 | loop fusion | flops 2738176 | bytes 5562368 | tf_op jit(solution)/shard_map/reduce_sum | solution.py:93
  169.1 37.4 %all_gather.7 = bf16[64,8,256]{2,1,0:T(8,128)(2,1)S(1)} all-gather(bf16[1,8,256]{2,1,0:T(8,128)(2,1)S(1)} %bitcast_select_fusion), channel_id=1, replica_groups=mesh['req'=64,'tp'=8] {'req'}, dimensions={0}, use_global_device_ids=true | all-gather | bytes 266240 | tf_op jit(solution)/shard_map/all_gather | solution.py:130
  207.1 44.1 %all-gather.2.cloned.1.call-done = bf16[64,28,512]{2,1,0:T(8,128)(2,1)} async-done(((bf16[1,28,512]{2,1,0:T(8,128)(2,1)}), bf16[64,28,512]{2,1,0:T(8,128)(2,1)}) %all-gather.2.cloned.1.call-update) | async-done | bytes 1835024 | tf_op jit(solution)/shard_map/all_gather | solution.py:122
  251.2 3.7 %fusion.2 = bf16[64,28,64]{2,0,1:T(8,128)(2,1)S(1)} fusion(bf16[64,28,512]{2,1,0:T(8,128)(2,1)} %all-gather.2.cloned.1.call-done, bf16[512,64]{0,1:T(8,128)(2,1)S(1)} %copy-done), kind=kOutput, calls=%fused_computation.10 | convolution fusion | flops 117555200 | bytes 2129920 | tf_op jit(solution)/shard_map/dot_general | solution.py:124
  255.3 1.1 reshape.680
  256.5 4.2 %gather_fusion.5 = bf16[768,256]{1,0:T(8,128)(2,1)S(1)} fusion(bf16[3,8,256]{2,1,0:T(8,128)(2,1)S(1)} %gather_fusion.4, s32[768]{0:T(1024)S(1)} %reshape.667), kind=kCustom, calls=%fused_computation.5 | custom fusion | bytes 792576 | tf_op jit(solution)/shard_map/jit(take_along_axis)/gather | solution.py:135
  260.7 1.0 select_select_fusion
  261.8 34.0 %reduce-scatter.4.cloned.1.call-done = bf16[8,1792]{1,0:T(8,128)(2,1)} async-done(((bf16[64,1792]{1,0:T(8,128)(2,1)}), bf16[8,1792]{1,0:T(8,128)(2,1)}) %reduce-scatter.4.cloned.1.call-update) | async-done | bytes 28688
  295.7 0.9 reshape.681
  296.6 0.6 copy.162
  (91 shorter events, 8.5 us)
Async XLA Ops:
  7.2 244.1 %copy-start = (bf16[512,64]{0,1:T(8,128)(2,1)S(1)}, bf16[512,64]{0,1:T(8,128)(2,1)}, u32[]{:S(2)}) copy-start(bf16[512,64]{0,1:T(8,128)(2,1)} %param.15) | copy-start | bytes 196612
  9.6 10.8 %copy-start.2 = (bf16[3,256,256]{2,1,0:T(8,128)(2,1)S(1)}, bf16[3,256,256]{2,1,0:T(8,128)(2,1)}, u32[]{:S(2)}) copy-start(bf16[3,256,256]{2,1,0:T(8,128)(2,1)} %param.12) | copy-start | bytes 1179652
  9.6 11.0 %copy-start.15 = (s32[3,2]{0,1:T(2,128)S(1)}, s32[3,2]{0,1:T(2,128)}, u32[]{:S(2)}) copy-start(s32[3,2]{0,1:T(2,128)} %param.13) | copy-start | bytes 76
  9.6 11.1 %copy-start.8 = (s32[64,8]{0,1:T(8,128)S(1)}, s32[64,8]{0,1:T(8,128)}, u32[]{:S(2)}) copy-start(s32[64,8]{0,1:T(8,128)} %param.11) | copy-start | bytes 6148
  9.6 11.7 %copy-start.1 = (s32[64]{0:T(128)S(1)}, s32[64]{0:T(128)}, u32[]{:S(2)}) copy-start(s32[64]{0:T(128)} %param.14) | copy-start | bytes 772
  9.6 60.3 %all-to-all-start = ((bf16[64,28,512]{2,1,0:T(8,128)(2,1)}), bf16[64,28,512]{2,1,0:T(8,128)(2,1)S(1)}, u32[]{:S(2)}, u32[]{:S(2)}) async-start(bf16[64,28,512]{2,1,0:T(8,128)(2,1)} %tile.10), calls=%async_computation | async-start | bytes 4194304 | tf_op jit(solution)/shard_map/all_to_all | solution.py:14
  20.6 50.3 %copy-start.9 = (s32[3]{0:T(128)}, s32[3]{0:T(128)S(1)}, u32[]{:S(2)}) copy-start(s32[3]{0:T(128)S(1)} %get-tuple-element.14) | copy-start | bytes 40
  21.9 48.6 %copy-start.11 = (s32[3]{0:T(128)}, s32[3]{0:T(128)S(1)}, u32[]{:S(2)}) copy-start(s32[3]{0:T(128)S(1)} %gather_fusion) | copy-start | bytes 40
  72.4 16.4 %all-to-all-start.1 = ((bf16[64,28,4]{1,2,0:T(4,128)(2,1)}), bf16[64,28,4]{1,2,0:T(4,128)(2,1)S(1)}, u32[]{:S(2)}, u32[]{:S(2)}) async-start(bf16[64,28,4]{1,2,0:T(4,128)(2,1)} %copy.129), calls=%async_computation.1 | async-start | bytes 131072 | tf_op jit(solution)/shard_map/all_to_all | solution.py:79
  88.8 14.8 %all-to-all-start.3 = ((bf16[64,28,4]{1,2,0:T(4,128)(2,1)}), bf16[64,28,4]{1,2,0:T(4,128)(2,1)S(1)}, u32[]{:S(2)}, u32[]{:S(2)}) async-start(bf16[64,28,4]{1,2,0:T(4,128)(2,1)} %copy.150), calls=%async_computation.3 | async-start | bytes 131072 | tf_op jit(solution)/shard_map/all_to_all | solution.py:82
  103.6 10.8 %copy-start.4 = (bf16[1,28,512]{2,1,0:T(8,128)(2,1)S(1)}, bf16[1,28,512]{2,1,0:T(8,128)(2,1)}, u32[]{:S(2)}) copy-start(bf16[1,28,512]{2,1,0:T(8,128)(2,1)} %param.8) | copy-start | bytes 86020
  103.6 10.8 %copy-start.3 = (bf16[1,28,256]{2,1,0:T(8,128)(2,1)S(1)}, bf16[1,28,256]{2,1,0:T(8,128)(2,1)}, u32[]{:S(2)}) copy-start(bf16[1,28,256]{2,1,0:T(8,128)(2,1)} %param.9) | copy-start | bytes 43012
  103.6 10.8 %copy-start.16 = (s32[1,28]{1,0:T(1,128)S(1)}, s32[1,28]{1,0:T(1,128)}, u32[]{:S(2)}) copy-start(s32[1,28]{1,0:T(1,128)} %param.10) | copy-start | bytes 340
  103.6 60.0 %all-to-all-start.2 = ((bf16[64,28,512]{2,1,0:T(8,128)(2,1)}), bf16[64,28,512]{2,1,0:T(8,128)(2,1)S(1)}, u32[]{:S(2)}, u32[]{:S(2)}) async-start(bf16[64,28,512]{2,1,0:T(8,128)(2,1)} %reshape.679), calls=%async_computation.2 | async-start | bytes 4194304 | tf_op jit(solution)/shard_map/all_to_all | solution.py:85
  114.1 137.2 %all-gather.2.cloned.1.call-start = ((), (), s32[]{:S(2)}) async-start(), calls=%async_computation.5 | async-start | bytes 2129920 | tf_op jit(solution)/shard_map/all_gather | solution.py:122
  129.2 37.7 %copy-start.5 = (f32[28,4]{1,0:T(8,128)S(1)}, f32[28,4]{1,0:T(8,128)}, u32[]{:S(2)}) copy-start(f32[28,4]{1,0:T(8,128)} %copy.154) | copy-start | bytes 1348
  129.2 37.8 %copy-start.6 = (f32[28,4]{1,0:T(8,128)S(1)}, f32[28,4]{1,0:T(8,128)}, u32[]{:S(2)}) copy-start(f32[28,4]{1,0:T(8,128)} %copy.148) | copy-start | bytes 1348
  129.2 37.9 %copy-start.7 = (f32[28,4]{1,0:T(8,128)S(1)}, f32[28,4]{1,0:T(8,128)}, u32[]{:S(2)}) copy-start(f32[28,4]{1,0:T(8,128)} %copy.144) | copy-start | bytes 1348
  168.0 127.7 %reduce-scatter.4.cloned.1.call-start = ((), (), s32[]{:S(2)}) async-start(), calls=%async_computation.6 | async-start | bytes 258048
  207.1 49.3 %copy-start.10 = (s32[3]{0:T(128)S(1)}, s32[3]{0:T(128)}, u32[]{:S(2)}) copy-start(s32[3]{0:T(128)} %copy-done.9) | copy-start | bytes 40
  207.1 49.3 %copy-start.12 = (s32[3]{0:T(128)S(1)}, s32[3]{0:T(128)}, u32[]{:S(2)}) copy-start(s32[3]{0:T(128)} %copy-done.11) | copy-start | bytes 40
  256.4 4.3 %copy-start.13 = (pred[3,256]{1,0:T(4,128)(4,1)S(1)}, pred[3,256]{1,0:T(4,128)(4,1)}, u32[]{:S(2)}) copy-start(pred[3,256]{1,0:T(4,128)(4,1)} %get-tuple-element.9) | copy-start | bytes 2308
  256.4 4.4 %copy-start.14 = (pred[3,256]{1,0:T(4,128)(4,1)S(1)}, pred[3,256]{1,0:T(4,128)(4,1)}, u32[]{:S(2)}) copy-start(pred[3,256]{1,0:T(4,128)(4,1)} %get-tuple-element.11) | copy-start | bytes 2308
Sparse Core Ops, SparseCore 0:
  168.1 83.0 all-gather.1
  256.5 39.1 reduce-scatter.3
